TPU v7x, 128 devices: a whole 4x4x4 slice. The times are simulated.
128 devices in a mesh: prow: 8 (over x, y_lo), pcol: 16 (over y_hi, z, core).
Axes of the slice: x: 4, y: 4 (y_hi: 2, y_lo: 2; y = y_hi * 2 + y_lo), z: 4, core: 2. Of those that a mesh axis runs over, the one named last changes fastest.
Arguments:
- inverse_top: bfloat16 [128, 128, 128, 128], P('prow', 'pcol'), may hold values from -6 to 6
- rows_one: int32 [16, 64], replicated, may hold values from 0 to 127, as said below
- panel_one: bfloat16 [16, 64, 128, 128], P('pcol', 'prow'), may hold values from -0.0625 to 0.0625
- base_one: float32 [16, 128, 128], P('pcol'), may hold values from -6 to 6
- parent_two: int32 [16], replicated, may hold values from 0 to 15
- order_two: int32 [16, 64], replicated, may hold values from 0 to 63, as said below
- panel_two: bfloat16 [16, 64, 128, 128], P('pcol', 'prow'), may hold values from -0.0625 to 0.0625
- link_two: bfloat16 [16, 128, 128], P('pcol'), may hold values from -0.5 to 0.5
- base_two: float32 [16, 128, 128], P('pcol'), may hold values from -6 to 6
Outputs:
- column_one: bfloat16 [16, 64, 128, 128], P('pcol', 'prow')
- diagonal_one: bfloat16 [16, 128, 128], P('pcol')
- column_two: bfloat16 [16, 64, 128, 128], P('pcol', 'prow')
- upper_two: bfloat16 [16, 128, 128], P('pcol')
- diagonal_two: bfloat16 [16, 128, 128], P('pcol')
Inputs may be any that keep to these rules, and one draw needn't show every extreme that they name: For every supernode k and process row p, rows_one[k, p * 8] to rows_one[k, p * 8 + 7] are 8 distinct ancestors between p * 16 and p * 16 + 15. In every draw some process column c holds 8 ancestors (ancestor // 8 == c) of every level-one supernode. Each block order_two[k, p * 8] to order_two[k, p * 8 + 7] is a permutation of p * 8 to p * 8 + 7.
All inputs are finite; a program needn't handle non-finite values.
Results may differ from a plain program's by a relative error of at most 0.024.
Values may be sent and summed in bfloat16 or wider, within the bound.
A program may use at most 192 MiB of HBM per device.

v0:
```python
import jax
import jax.numpy as jnp
from jax import lax
from jax.sharding import PartitionSpec as P


def slot_positions(rows_all, dests, width, capacity):
    owner = rows_all // width
    length = rows_all.shape[1]
    positions = jnp.arange(length, dtype=jnp.int32)
    same_owner = owner[:, :, None] == owner[:, None, :]
    earlier = positions[None, None, :] < positions[None, :, None]
    ranking = jnp.sum(jnp.logical_and(same_owner, earlier), axis=2)
    slot_ids = jnp.arange(capacity, dtype=jnp.int32)
    matches = jnp.logical_and(
        owner[None, :, None, :] == dests[:, None, None, None],
        ranking[None, :, None, :] == slot_ids[None, None, :, None],
    )
    where_at = jnp.sum(jnp.where(matches, positions, 0), axis=3)
    present = jnp.any(matches, axis=3)
    return (where_at, present)


def pack_panels(full_panel, my_rows, width, capacity, columns):
    where_at, present = slot_positions(
        my_rows, jnp.arange(columns, dtype=jnp.int32), width, capacity
    )
    children = jnp.arange(my_rows.shape[0], dtype=jnp.int32)[None, :, None]
    selected = full_panel[children, where_at]
    return jnp.where(present[:, :, :, None, None], selected, jnp.zeros((), selected.dtype))


def local_indices(rows_all, prow_at, pcol_at, per_row, height, width):
    where_at, present = slot_positions(rows_all, jnp.reshape(pcol_at, (1,)), width, per_row)
    targets = jnp.take_along_axis(rows_all, where_at[0], axis=1)
    col_local = jnp.where(present[0], targets - pcol_at * width, 0)
    row_local = lax.dynamic_slice_in_dim(rows_all, prow_at * per_row, per_row, 1) - prow_at * height
    return (row_local, col_local)


def tile_products(inverse_local, received, row_local, col_local):
    blocks = inverse_local[row_local[:, :, None], col_local[:, None, :]]
    return jnp.einsum("kabij,kbjl->kail", blocks, received, preferred_element_type=jnp.float32)


def flatten_received(received):
    return received.reshape((received.shape[0] * received.shape[1],) + received.shape[2:])


def local(
    inverse_top, rows_one, panel_one, base_one, parent_two, order_two, panel_two, link_two, base_two
):
    per_col = panel_one.shape[0]
    per_row = panel_one.shape[1]
    height = inverse_top.shape[0]
    width = inverse_top.shape[1]
    columns = lax.axis_size("pcol")
    prow_at = lax.axis_index("prow")
    pcol_at = lax.axis_index("pcol")
    rows_two = jnp.take_along_axis(rows_one[parent_two], order_two, axis=1)
    mine_one = lax.dynamic_slice_in_dim(rows_one, pcol_at * per_col, per_col, 0)
    mine_two = lax.dynamic_slice_in_dim(rows_two, pcol_at * per_col, per_col, 0)
    row_one, col_one = local_indices(rows_one, prow_at, pcol_at, per_row, height, width)
    row_two, col_two = local_indices(rows_two, prow_at, pcol_at, per_row, height, width)
    full_one = lax.all_gather(panel_one, "prow", axis=1, tiled=True)
    outgoing_one = pack_panels(full_one, mine_one, width, per_row, columns)
    received_one = lax.all_to_all(outgoing_one, "pcol", split_axis=0, concat_axis=0, tiled=True)
    flat_one = flatten_received(received_one)
    summed_one = lax.psum_scatter(
        tile_products(inverse_top, flat_one, row_one, col_one).astype(jnp.bfloat16),
        "pcol",
        scatter_dimension=0,
        tiled=True,
    ).astype(jnp.float32)
    full_two = lax.all_gather(panel_two, "prow", axis=1, tiled=True)
    outgoing_two = pack_panels(full_two, mine_two, width, per_row, columns)
    received_two = lax.all_to_all(outgoing_two, "pcol", split_axis=0, concat_axis=0, tiled=True)
    flat_two = flatten_received(received_two)
    summed_two = lax.psum_scatter(
        tile_products(inverse_top, flat_two, row_two, col_two).astype(jnp.bfloat16),
        "pcol",
        scatter_dimension=0,
        tiled=True,
    ).astype(jnp.float32)
    column_one = (-summed_one).astype(jnp.bfloat16)
    diag_part = jnp.einsum(
        "cmij,cmil->cjl", panel_one, column_one, preferred_element_type=jnp.float32
    )
    diagonal_one = (
        base_one - lax.psum(diag_part.astype(jnp.bfloat16), "prow").astype(jnp.float32)
    ).astype(jnp.bfloat16)
    all_cols, all_diag = (
        lax.all_gather(column_one, "pcol", axis=0, tiled=True),
        lax.all_gather(diagonal_one, "pcol", axis=0, tiled=True),
    )
    my_parent = lax.dynamic_slice_in_dim(parent_two, pcol_at * per_col, per_col, 0)
    my_order = (
        lax.dynamic_slice(order_two, (pcol_at * per_col, prow_at * per_row), (per_col, per_row))
        - prow_at * per_row
    )
    near_cols = all_cols[my_parent[:, None], my_order]
    near_diag = all_diag[my_parent]
    carried = jnp.einsum("cmij,cjl->cmil", near_cols, link_two, preferred_element_type=jnp.float32)
    column_two = (-(summed_two + carried)).astype(jnp.bfloat16)
    upper_part = jnp.einsum(
        "cmij,cmil->cjl", near_cols, panel_two, preferred_element_type=jnp.float32
    )
    parent_term = jnp.einsum(
        "cij,cjl->cil", near_diag, link_two, preferred_element_type=jnp.float32
    )
    upper_total = lax.psum(upper_part.astype(jnp.bfloat16), "prow").astype(jnp.float32)
    upper_two = (-(parent_term + upper_total)).astype(jnp.bfloat16)
    lower_part = jnp.einsum(
        "cmij,cmil->cjl", panel_two, column_two, preferred_element_type=jnp.float32
    )
    lower_total = lax.psum(lower_part.astype(jnp.bfloat16), "prow").astype(jnp.float32)
    link_term = jnp.einsum("cij,cil->cjl", link_two, upper_two, preferred_element_type=jnp.float32)
    diagonal_two = (base_two - link_term - lower_total).astype(jnp.bfloat16)
    return (column_one, diagonal_one, column_two, upper_two, diagonal_two)


def solution(mesh):
    return jax.shard_map(
        local,
        mesh=mesh,
        in_specs=(
            P("prow", "pcol", None, None),
            P(),
            P("pcol", "prow", None, None),
            P("pcol", None, None),
            P(),
            P(),
            P("pcol", "prow", None, None),
            P("pcol", None, None),
            P("pcol", None, None),
        ),
        out_specs=(
            P("pcol", "prow", None, None),
            P("pcol", None, None),
            P("pcol", "prow", None, None),
            P("pcol", None, None),
            P("pcol", None, None),
        ),
        check_vma=False,
    )
```

profile of v0, /device:TPU:1, one launch (start us, length us, event | category | flops | bytes accessed | tf_op | source)
XLA Modules:
  0.0 586.9 jit_solution(2834945553307721107)
XLA Ops:
  7.2 0.7 all-gather.4.cloned.1.call-update
  7.9 0.7 fusion.64
  8.6 0.2 convert_reduce_fusion.3
  8.8 0.4 fusion.28
  9.4 0.1 reshape.639
  9.4 0.4 and_reduce_fusion.1
  9.8 52.7 %all-gather.4.cloned.1.call-done = bf16[1,64,128,128]{3,2,0,1:T(8,128)(2,1)} async-done(((bf16[1,8,128,128]{3,2,0,1:T(8,128)(2,1)}), bf16[1,64,128,128]{3,2,0,1:T(8,128)(2,1)}) %all-gather.4.cloned.1.call-update) | async-done | bytes 2097168 | tf_op jit(solution)/shard_map/all_gather | solution.py:65
  62.6 4.6 gather_fusion.1
  67.2 4.6 broadcast_select_fusion.1
  71.8 8.7 %all-to-all-start = ((bf16[16,1,8,128,128]{4,3,2,1,0:T(8,128)(2,1)}), bf16[16,1,8,128,128]{4,3,2,1,0:T(8,128)(2,1)}, u32[]{:S(2)}, u32[]{:S(2)}) async-start(bf16[16,1,8,128,128]{4,3,2,1,0:T(8,128)(2,1)} %broadcast_select_fusion.1), calls=%async_computation | async-start | bytes 8388608 | tf_op jit(solution)/shard_map/all_to_all | solution.py:67
  80.5 0.6 gather_fusion.2
  81.2 7.1 %gather_fusion.6 = s32[1024]{0:T(1024)S(1)} fusion(s32[16,64]{1,0:T(8,128)S(1)} %gather_fusion.2, s32[1024]{0:T(1024)S(1)} %reshape.675), kind=kCustom, calls=%fused_computation.8 | custom fusion | bytes 16384 | tf_op jit(solution)/shard_map/jit(take_along_axis)/gather | solution.py:60
  88.3 0.9 convert_reduce_fusion
  89.3 0.3 select_reduce_fusion.1
  89.8 0.1 reshape.701
  89.9 1.3 gather_fusion.7
  91.2 0.1 reshape.704
  91.3 0.1 fusion.45
  91.3 0.4 fusion.31
  91.7 0.1 broadcast_or_fusion.1
  91.8 0.1 reshape.631
  91.9 23.3 %gather_fusion = bf16[1024,128,128]{2,1,0:T(8,128)(2,1)} fusion(bf16[16,8,128,128]{3,2,1,0:T(8,128)(2,1)} %param.11, s32[1024]{0:T(1024)S(1)} %reshape.631), kind=kCustom, calls=%fused_computation.2 | custom fusion | bytes 67117056 | tf_op jit(solution)/shard_map/gather | solution.py:42
  115.2 20.5 %all-to-all-done = bf16[16,1,8,128,128]{4,3,2,1,0:T(8,128)(2,1)} async-done(((bf16[16,1,8,128,128]{4,3,2,1,0:T(8,128)(2,1)}), bf16[16,1,8,128,128]{4,3,2,1,0:T(8,128)(2,1)}, u32[]{:S(2)}, u32[]{:S(2)}) %all-to-all-start) | async-done | bytes 4194336 | tf_op jit(solution)/shard_map/all_to_all | solution.py:67
  135.7 17.7 %bitcast_convert_fusion.1 = bf16[16,8,128,128]{3,2,1,0:T(8,128)(2,1)} fusion(bf16[16,8,8,128,128]{4,3,2,1,0:T(8,128)(2,1)} %bitcast.161, bf16[16,1,8,128,128]{4,3,2,1,0:T(8,128)(2,1)} %all-to-all-done), kind=kOutput, calls=%fused_computation.10 | convolution fusion | flops 4297064448 | bytes 41943040 | tf_op jit(solution)/shard_map/kabij,kbjl->kail/dot_general | solution.py:43
  153.5 0.7 all-gather.6.cloned.1.call-update
  154.3 0.2 convert_reduce_fusion.2
  154.5 85.3 %reduce-scatter.3.cloned.1.call-done = bf16[1,8,128,128]{3,2,1,0:T(8,128)(2,1)} async-done(((bf16[16,8,128,128]{3,2,1,0:T(8,128)(2,1)}), bf16[1,8,128,128]{3,2,1,0:T(8,128)(2,1)}) %reduce-scatter.3.cloned.1.call-update) | async-done | bytes 262160 | tf_op jit(solution)/shard_map/reduce_scatter | solution.py:69
  239.8 1.7 negate_convert_fusion
  241.5 0.4 fusion.29
  242.0 0.1 reshape.661
  242.1 0.4 and_reduce_fusion
  242.5 48.9 %all-gather.6.cloned.1.call-done = bf16[1,64,128,128]{3,2,0,1:T(8,128)(2,1)} async-done(((bf16[1,8,128,128]{3,2,0,1:T(8,128)(2,1)}), bf16[1,64,128,128]{3,2,0,1:T(8,128)(2,1)}) %all-gather.6.cloned.1.call-update) | async-done | bytes 2097168 | tf_op jit(solution)/shard_map/all_gather | solution.py:75
  291.4 4.6 gather_fusion.4
  296.0 4.5 broadcast_select_fusion
  300.4 8.5 %all-to-all-start.1 = ((bf16[16,1,8,128,128]{4,3,2,1,0:T(8,128)(2,1)}), bf16[16,1,8,128,128]{4,3,2,1,0:T(8,128)(2,1)}, u32[]{:S(2)}, u32[]{:S(2)}) async-start(bf16[16,1,8,128,128]{4,3,2,1,0:T(8,128)(2,1)} %broadcast_select_fusion), calls=%async_computation.2 | async-start | bytes 8388608 | tf_op jit(solution)/shard_map/all_to_all | solution.py:77
  309.0 0.2 reduce-scatter.5.cloned.1.call-start
  309.2 0.3 select_reduce_fusion
  309.7 0.1 reshape.706
  309.8 1.3 gather_fusion.8
  311.1 0.1 reshape.709
  311.2 0.1 fusion.49
  311.3 0.4 fusion.33
  311.6 0.1 broadcast_or_fusion
  311.7 0.1 reshape.653
  311.8 23.3 %gather_fusion.3 = bf16[1024,128,128]{2,1,0:T(8,128)(2,1)} fusion(bf16[16,8,128,128]{3,2,1,0:T(8,128)(2,1)} %param.11, s32[1024]{0:T(1024)S(1)} %reshape.653), kind=kCustom, calls=%fused_computation.5 | custom fusion | bytes 67117056 | tf_op jit(solution)/shard_map/gather | solution.py:42
  335.1 34.6 %all-to-all-done.1 = bf16[16,1,8,128,128]{4,3,2,1,0:T(8,128)(2,1)} async-done(((bf16[16,1,8,128,128]{4,3,2,1,0:T(8,128)(2,1)}), bf16[16,1,8,128,128]{4,3,2,1,0:T(8,128)(2,1)}, u32[]{:S(2)}, u32[]{:S(2)}) %all-to-all-start.1) | async-done | bytes 4194336 | tf_op jit(solution)/shard_map/all_to_all | solution.py:77
  369.8 17.9 %bitcast_convert_fusion = bf16[16,8,128,128]{3,2,1,0:T(8,128)(2,1)} fusion(bf16[16,8,8,128,128]{4,3,2,1,0:T(8,128)(2,1)} %bitcast.162, bf16[16,1,8,128,128]{4,3,2,1,0:T(8,128)(2,1)} %all-to-all-done.1), kind=kOutput, calls=%fused_computation.9 | convolution fusion | flops 4297064448 | bytes 41943040 | tf_op jit(solution)/shard_map/kabij,kbjl->kail/dot_general | solution.py:43
  387.8 0.7 dynamic_slice.23
  390.3 0.1 fusion.63
  390.4 0.9 fusion.22
  391.3 2.8 gather_fusion.5
  394.1 0.9 fusion.21
  395.0 80.1 %reduce-scatter.5.cloned.1.call-done = bf16[1,8,128,128]{3,2,1,0:T(8,128)(2,1)} async-done(((bf16[16,8,128,128]{3,2,1,0:T(8,128)(2,1)}), bf16[1,8,128,128]{3,2,1,0:T(8,128)(2,1)}) %reduce-scatter.5.cloned.1.call-update) | async-done | bytes 262160 | tf_op jit(solution)/shard_map/reduce_scatter | solution.py:79
  475.1 1.2 fusion.10
  476.3 0.9 fusion.20
  477.2 0.1 copy.193
  478.6 0.1 copy.201
  479.3 66.1 %all-reduce.6.cloned.1.call-done = (bf16[1,128,128]{1,2,0:T(8,128)(2,1)}, bf16[1,128,128]{2,1,0:T(8,128)(2,1)}, bf16[1,128,128]{1,2,0:T(8,128)(2,1)}) async-done(((bf16[1,128,128]{1,2,0:T(8,128)(2,1)}, bf16[1,128,128]{2,1,0:T(8,128)(2,1)}, bf16[1,128,128]{1,2,0:T(8,128)(2,1)}), (bf16[1,128,128]{1,2,0:T(8,128)(2,1)}, bf16[1,128,128]{2,1,0:T(8,128)(2,1)}, ...) | async-done | bytes 98320 | tf_op jit(solution)/shard_map/psum | solution.py:90
  545.4 0.8 subtract_convert_fusion
  546.2 0.1 copy.203
  546.3 31.2 %all_gather.15 = bf16[16,128,128]{2,1,0:T(8,128)(2,1)S(1)} all-gather(bf16[1,128,128]{2,1,0:T(8,128)(2,1)S(1)} %copy.203), channel_id=1, replica_groups=mesh['prow'=8,'pcol'=16] {'pcol'}, dimensions={0}, use_global_device_ids=true | all-gather | bytes 557056 | tf_op jit(solution)/shard_map/all_gather | solution.py:94
  577.5 0.9 fusion.16
  578.4 1.0 fusion.15
  579.4 0.7 copy.204
  (68 shorter events, 1.3 us)
Async XLA Ops:
  7.2 468.0 %copy-start = (bf16[1,128,128]{2,1,0:T(8,128)(2,1)S(1)}, bf16[1,128,128]{2,1,0:T(8,128)(2,1)}, u32[]{:S(2)}) copy-start(bf16[1,128,128]{2,1,0:T(8,128)(2,1)} %param.18) | copy-start | bytes 98308
  7.2 55.4 %all-gather.4.cloned.1.call-start = ((), (), s32[]{:S(2)}) async-start(), calls=%async_computation.4 | async-start | bytes 2359296 | tf_op jit(solution)/shard_map/all_gather | solution.py:65
  71.7 8.7 %copy-start.11 = (s32[16]{0:T(128)S(1)}, s32[16]{0:T(128)}, u32[]{:S(2)}) copy-start(s32[16]{0:T(128)} %param.15) | copy-start | bytes 196
  71.8 8.7 %copy-start.1 = (s32[16,64]{1,0:T(8,128)S(1)}, s32[16,64]{1,0:T(8,128)}, u32[]{:S(2)}) copy-start(s32[16,64]{1,0:T(8,128)} %param.12) | copy-start | bytes 12292
  71.8 9.3 %copy-start.10 = (s32[16,64]{1,0:T(8,128)S(1)}, s32[16,64]{1,0:T(8,128)}, u32[]{:S(2)}) copy-start(s32[16,64]{1,0:T(8,128)} %param.16) | copy-start | bytes 12292
  71.8 64.0 %all-to-all-start = ((bf16[16,1,8,128,128]{4,3,2,1,0:T(8,128)(2,1)}), bf16[16,1,8,128,128]{4,3,2,1,0:T(8,128)(2,1)}, u32[]{:S(2)}, u32[]{:S(2)}) async-start(bf16[16,1,8,128,128]{4,3,2,1,0:T(8,128)(2,1)} %broadcast_select_fusion.1), calls=%async_computation | async-start | bytes 8388608 | tf_op jit(solution)/shard_map/all_to_all | solution.py:67
  80.4 159.4 %reduce-scatter.3.cloned.1.call-start = ((), (), s32[]{:S(2)}) async-start(), calls=%async_computation.5 | async-start | bytes 4456448 | tf_op jit(solution)/shard_map/reduce_scatter | solution.py:69
  153.5 137.9 %all-gather.6.cloned.1.call-start = ((), (), s32[]{:S(2)}) async-start(), calls=%async_computation.6 | async-start | bytes 2359296 | tf_op jit(solution)/shard_map/all_gather | solution.py:75
  154.2 237.1 %all-gather.8.cloned.1.call-start = ((), (), s32[]{:S(2)}) async-start(), calls=%async_computation.8 | async-start | bytes 4456448 | tf_op jit(solution)/shard_map/all_gather | solution.py:93
  300.4 69.3 %all-to-all-start.1 = ((bf16[16,1,8,128,128]{4,3,2,1,0:T(8,128)(2,1)}), bf16[16,1,8,128,128]{4,3,2,1,0:T(8,128)(2,1)}, u32[]{:S(2)}, u32[]{:S(2)}) async-start(bf16[16,1,8,128,128]{4,3,2,1,0:T(8,128)(2,1)} %broadcast_select_fusion), calls=%async_computation.2 | async-start | bytes 8388608 | tf_op jit(solution)/shard_map/all_to_all | solution.py:77
  309.0 166.2 %reduce-scatter.5.cloned.1.call-start = ((), (), s32[]{:S(2)}) async-start(), calls=%async_computation.7 | async-start | bytes 4456448 | tf_op jit(solution)/shard_map/reduce_scatter | solution.py:79
  387.7 2.7 copy-start.3
  387.7 2.7 copy-start.5
  387.7 6.4 %copy-start.2 = (bf16[1,8,128,128]{3,2,1,0:T(8,128)(2,1)S(1)}, bf16[1,8,128,128]{3,2,1,0:T(8,128)(2,1)}, u32[]{:S(2)}) copy-start(bf16[1,8,128,128]{3,2,1,0:T(8,128)(2,1)} %param.17) | copy-start | bytes 786436
  387.7 89.6 %copy-start.8 = (f32[1,128,128]{2,1,0:T(8,128)S(1)}, f32[1,128,128]{2,1,0:T(8,128)}, u32[]{:S(2)}) copy-start(f32[1,128,128]{2,1,0:T(8,128)} %param.14) | copy-start | bytes 196612
  387.7 90.9 %copy-start.9 = (f32[1,128,128]{2,1,0:T(8,128)S(1)}, f32[1,128,128]{2,1,0:T(8,128)}, u32[]{:S(2)}) copy-start(f32[1,128,128]{2,1,0:T(8,128)} %param.19) | copy-start | bytes 196612
  387.7 157.7 %all-reduce.6.cloned.1.call-start = ((), (), s32[]{:S(2)}) async-start(), calls=%async_computation.9 | async-start | bytes 196608 | tf_op jit(solution)/shard_map/psum | solution.py:90
  476.3 103.8 %copy-start.4 = (bf16[1,8,128,128]{3,2,1,0:T(8,128)(2,1)}, bf16[1,8,128,128]{3,2,1,0:T(8,128)(2,1)S(1)}, u32[]{:S(2)}) copy-start(bf16[1,8,128,128]{3,2,1,0:T(8,128)(2,1)S(1)} %fusion.10) | copy-start | bytes 786436
  546.3 33.8 %copy-start.6 = (bf16[1,128,128]{2,1,0:T(8,128)(2,1)}, bf16[1,128,128]{2,1,0:T(8,128)(2,1)S(1)}, u32[]{:S(2)}) copy-start(bf16[1,128,128]{2,1,0:T(8,128)(2,1)S(1)} %copy.203) | copy-start | bytes 98308
  578.4 1.7 copy-start.7
Sparse Core Ops, SparseCore 0:
  9.6 52.8 all-gather.3
  153.6 86.1 reduce-scatter.2
  241.4 49.8 all-gather.5
  294.2 92.8 all-gather.7
  391.0 84.0 reduce-scatter.4
  478.3 67.1 all-reduce.5
where the time goes:
time: 588 us; the launch traced here: 587 us
  waiting for transfers between devices  390 us (66%)
  local copies, waits for them, and re-layouts  71.9 us (12%)
  matrix products  41.3 us (7%)
  blocking collectives  31.2 us (5%)
  between operations  18.2 us (3%)
  starting transfers between devices  17.6 us (3%)
  other arithmetic  17 us (3%)
    reduce_scatter x1, waiting for transfers between devices, local(): lax.psum_scatter(tile_products(inverse_top, flat_one, row_one, col_one).a...  85.3 us
    reduce_scatter x1, waiting for transfers between devices, local(): lax.psum_scatter(tile_products(inverse_top, flat_two, row_two, col_two).a...  80.1 us
    psum x1, waiting for transfers between devices, local(): lax.psum(diag_part.astype(jnp.bfloat16), 'prow').astype(jnp.float32)  66.1 us
    all_gather x1, waiting for transfers between devices, local(): full_one = lax.all_gather(panel_one, 'prow', axis=1, tiled=True)  52.7 us
    all_gather x1, waiting for transfers between devices, local(): full_two = lax.all_gather(panel_two, 'prow', axis=1, tiled=True)  48.9 us
    gather x2, local copies, waits for them, and re-layouts, tile_products(): blocks = inverse_local[row_local[:, :, None], col_local[:, None, :]]  46.6 us
    dot_general x2, matrix products, tile_products(): jnp.einsum('kabij,kbjl->kail', blocks, received, preferred_element_type=j...  35.6 us
    all_to_all x1, waiting for transfers between devices, local(): lax.all_to_all(outgoing_two, 'pcol', split_axis=0, concat_axis=0, tiled=T...  34.6 us
  transfers between devices with their start and end apart: 8, of which 7 were waited for; matrix products, arithmetic and copies ran while one was open for 17% of the time, Pallas kernels for 0%

commit v1 on v0

--- a/solution.py
+++ b/solution.py
@@ -87,7 +87,10 @@
         "cmij,cmil->cjl", panel_one, column_one, preferred_element_type=jnp.float32
     )
     diagonal_one = (
-        base_one - lax.psum(diag_part.astype(jnp.bfloat16), "prow").astype(jnp.float32)
+        base_one
+        - jnp.sum(lax.all_gather(diag_part.astype(jnp.bfloat16), "prow"), axis=0).astype(
+            jnp.float32
+        )
     ).astype(jnp.bfloat16)
     all_cols, all_diag = (
         lax.all_gather(column_one, "pcol", axis=0, tiled=True),

time: 588 us -> 562 us (0.956)
  waiting for transfers between devices: 390 us -> 346 us
  blocking collectives: 31.2 us -> 45.5 us
    reduce_scatter x1, waiting for transfers between devices: 80.1 us -> 57.1 us  [local(): lax.psum_scatter(tile_products(inverse_top, flat_two, row_two, col_two).a...]
    psum x1, waiting for transfers between devices: 66.1 us -> 44.9 us  [local(): lax.psum(upper_part.astype(jnp.bfloat16), 'prow').astype(jnp.float32)]
    all_gather x0 -> x1, blocking collectives: none -> 20.8 us  [local(): lax.all_gather(diag_part.astype(jnp.bfloat16), 'prow')]
    all_gather x1, blocking collectives: 31.2 us -> 24.7 us  [local(): lax.all_gather(diagonal_one, 'pcol', axis=0, tiled=True)]
  transfers between devices with their start and end apart: 8 -> 8, of which waited for: 7 -> 7; matrix products, arithmetic and copies ran while one was open for 17% -> 18% of each run, Pallas kernels for 0% -> 0%
where the time goes in v1:
time: 562 us; the launch traced here: 556 us
  waiting for transfers between devices  346 us (62%)
  local copies, waits for them, and re-layouts  72.1 us (13%)
  blocking collectives  45.5 us (8%)
  matrix products  40.7 us (7%)
  between operations  18.4 us (3%)
  starting transfers between devices  17.6 us (3%)
  other arithmetic  16.4 us (3%)
    reduce_scatter x1, waiting for transfers between devices, local(): lax.psum_scatter(tile_products(inverse_top, flat_one, row_one, col_one).a...  85.3 us
    reduce_scatter x1, waiting for transfers between devices, local(): lax.psum_scatter(tile_products(inverse_top, flat_two, row_two, col_two).a...  57.1 us
    all_gather x1, waiting for transfers between devices, local(): full_one = lax.all_gather(panel_one, 'prow', axis=1, tiled=True)  52.7 us
    all_gather x1, waiting for transfers between devices, local(): full_two = lax.all_gather(panel_two, 'prow', axis=1, tiled=True)  48.9 us
    gather x2, local copies, waits for them, and re-layouts, tile_products(): blocks = inverse_local[row_local[:, :, None], col_local[:, None, :]]  46.6 us
    psum x1, waiting for transfers between devices, local(): lax.psum(upper_part.astype(jnp.bfloat16), 'prow').astype(jnp.float32)  44.9 us
    dot_general x2, matrix products, tile_products(): jnp.einsum('kabij,kbjl->kail', blocks, received, preferred_element_type=j...  35.6 us
    all_to_all x1, waiting for transfers between devices, local(): lax.all_to_all(outgoing_two, 'pcol', split_axis=0, concat_axis=0, tiled=T...  34.6 us
  transfers between devices with their start and end apart: 8, of which 7 were waited for; matrix products, arithmetic and copies ran while one was open for 18% of the time, Pallas kernels for 0%

profile of v1, /device:TPU:1, one launch (start us, length us, event | category | flops | bytes accessed | tf_op | source)
XLA Modules:
  0.0 556.3 jit_solution(18304721176136836997)
XLA Ops:
  7.2 0.7 all-gather.5.cloned.1.call-update
  7.9 0.7 fusion.65
  8.6 0.2 convert_reduce_fusion.3
  8.8 0.4 fusion.28
  9.4 0.1 reshape.652
  9.4 0.4 and_reduce_fusion.1
  9.8 52.7 %all-gather.5.cloned.1.call-done = bf16[1,64,128,128]{3,2,0,1:T(8,128)(2,1)} async-done(((bf16[1,8,128,128]{3,2,0,1:T(8,128)(2,1)}), bf16[1,64,128,128]{3,2,0,1:T(8,128)(2,1)}) %all-gather.5.cloned.1.call-update) | async-done | bytes 2097168 | tf_op jit(solution)/shard_map/all_gather | solution.py:65
  62.6 4.6 gather_fusion.1
  67.2 4.6 broadcast_select_fusion.1
  71.8 8.7 %all-to-all-start = ((bf16[16,1,8,128,128]{4,3,2,1,0:T(8,128)(2,1)}), bf16[16,1,8,128,128]{4,3,2,1,0:T(8,128)(2,1)}, u32[]{:S(2)}, u32[]{:S(2)}) async-start(bf16[16,1,8,128,128]{4,3,2,1,0:T(8,128)(2,1)} %broadcast_select_fusion.1), calls=%async_computation | async-start | bytes 8388608 | tf_op jit(solution)/shard_map/all_to_all | solution.py:67
  80.5 0.6 gather_fusion.2
  81.2 7.1 %gather_fusion.6 = s32[1024]{0:T(1024)S(1)} fusion(s32[16,64]{1,0:T(8,128)S(1)} %gather_fusion.2, s32[1024]{0:T(1024)S(1)} %reshape.688), kind=kCustom, calls=%fused_computation.8 | custom fusion | bytes 16384 | tf_op jit(solution)/shard_map/jit(take_along_axis)/gather | solution.py:60
  88.3 0.9 convert_reduce_fusion
  89.3 0.3 select_reduce_fusion.1
  89.8 0.1 reshape.716
  89.9 1.3 gather_fusion.7
  91.2 0.1 reshape.719
  91.3 0.1 fusion.46
  91.3 0.4 fusion.32
  91.7 0.1 broadcast_or_fusion.1
  91.8 0.1 reshape.644
  91.9 23.3 %gather_fusion = bf16[1024,128,128]{2,1,0:T(8,128)(2,1)} fusion(bf16[16,8,128,128]{3,2,1,0:T(8,128)(2,1)} %param.11, s32[1024]{0:T(1024)S(1)} %reshape.644), kind=kCustom, calls=%fused_computation.2 | custom fusion | bytes 67117056 | tf_op jit(solution)/shard_map/gather | solution.py:42
  115.2 20.5 %all-to-all-done = bf16[16,1,8,128,128]{4,3,2,1,0:T(8,128)(2,1)} async-done(((bf16[16,1,8,128,128]{4,3,2,1,0:T(8,128)(2,1)}), bf16[16,1,8,128,128]{4,3,2,1,0:T(8,128)(2,1)}, u32[]{:S(2)}, u32[]{:S(2)}) %all-to-all-start) | async-done | bytes 4194336 | tf_op jit(solution)/shard_map/all_to_all | solution.py:67
  135.7 17.7 %bitcast_convert_fusion.1 = bf16[16,8,128,128]{3,2,1,0:T(8,128)(2,1)} fusion(bf16[16,8,8,128,128]{4,3,2,1,0:T(8,128)(2,1)} %bitcast.167, bf16[16,1,8,128,128]{4,3,2,1,0:T(8,128)(2,1)} %all-to-all-done), kind=kOutput, calls=%fused_computation.10 | convolution fusion | flops 4297064448 | bytes 41943040 | tf_op jit(solution)/shard_map/kabij,kbjl->kail/dot_general | solution.py:43
  153.5 0.7 all-gather.7.cloned.1.call-update
  154.3 0.2 convert_reduce_fusion.2
  154.5 85.3 %reduce-scatter.3.cloned.1.call-done = bf16[1,8,128,128]{3,2,1,0:T(8,128)(2,1)} async-done(((bf16[16,8,128,128]{3,2,1,0:T(8,128)(2,1)}), bf16[1,8,128,128]{3,2,1,0:T(8,128)(2,1)}) %reduce-scatter.3.cloned.1.call-update) | async-done | bytes 262160 | tf_op jit(solution)/shard_map/reduce_scatter | solution.py:69
  239.8 1.7 negate_convert_fusion
  241.5 0.4 fusion.29
  242.0 0.1 reshape.674
  242.1 0.4 and_reduce_fusion
  242.5 48.9 %all-gather.7.cloned.1.call-done = bf16[1,64,128,128]{3,2,0,1:T(8,128)(2,1)} async-done(((bf16[1,8,128,128]{3,2,0,1:T(8,128)(2,1)}), bf16[1,64,128,128]{3,2,0,1:T(8,128)(2,1)}) %all-gather.7.cloned.1.call-update) | async-done | bytes 2097168 | tf_op jit(solution)/shard_map/all_gather | solution.py:75
  291.4 4.6 gather_fusion.4
  296.0 4.5 broadcast_select_fusion
  300.5 8.5 %all-to-all-start.1 = ((bf16[16,1,8,128,128]{4,3,2,1,0:T(8,128)(2,1)}), bf16[16,1,8,128,128]{4,3,2,1,0:T(8,128)(2,1)}, u32[]{:S(2)}, u32[]{:S(2)}) async-start(bf16[16,1,8,128,128]{4,3,2,1,0:T(8,128)(2,1)} %broadcast_select_fusion), calls=%async_computation.2 | async-start | bytes 8388608 | tf_op jit(solution)/shard_map/all_to_all | solution.py:77
  309.0 0.2 reduce-scatter.5.cloned.1.call-start
  309.2 0.3 select_reduce_fusion
  309.7 0.1 reshape.721
  309.8 1.3 gather_fusion.8
  311.1 0.1 reshape.724
  311.2 0.1 fusion.50
  311.3 0.4 fusion.34
  311.7 0.1 reshape.666
  311.8 23.3 %gather_fusion.3 = bf16[1024,128,128]{2,1,0:T(8,128)(2,1)} fusion(bf16[16,8,128,128]{3,2,1,0:T(8,128)(2,1)} %param.11, s32[1024]{0:T(1024)S(1)} %reshape.666), kind=kCustom, calls=%fused_computation.5 | custom fusion | bytes 67117056 | tf_op jit(solution)/shard_map/gather | solution.py:42
  335.1 34.6 %all-to-all-done.1 = bf16[16,1,8,128,128]{4,3,2,1,0:T(8,128)(2,1)} async-done(((bf16[16,1,8,128,128]{4,3,2,1,0:T(8,128)(2,1)}), bf16[16,1,8,128,128]{4,3,2,1,0:T(8,128)(2,1)}, u32[]{:S(2)}, u32[]{:S(2)}) %all-to-all-start.1) | async-done | bytes 4194336 | tf_op jit(solution)/shard_map/all_to_all | solution.py:77
  369.8 17.9 %bitcast_convert_fusion = bf16[16,8,128,128]{3,2,1,0:T(8,128)(2,1)} fusion(bf16[16,8,8,128,128]{4,3,2,1,0:T(8,128)(2,1)} %bitcast.168, bf16[16,1,8,128,128]{4,3,2,1,0:T(8,128)(2,1)} %all-to-all-done.1), kind=kOutput, calls=%fused_computation.9 | convolution fusion | flops 4297064448 | bytes 41943040 | tf_op jit(solution)/shard_map/kabij,kbjl->kail/dot_general | solution.py:43
  387.8 0.6 dynamic_slice.23
  389.7 0.1 copy.189
  391.1 0.1 copy.197
  392.5 0.1 fusion.64
  392.6 0.3 fusion.22
  392.9 20.8 %all-gather = bf16[1024,128]{0,1:T(8,128)(2,1)S(1)} all-gather(bf16[128,128]{0,1:T(8,128)(2,1)S(1)} %fusion.22), channel_id=2, replica_groups=mesh['prow'=8,'pcol'=16] {'prow'}, dimensions={0}, use_global_device_ids=true | all-gather | bytes 294912 | tf_op jit(solution)/shard_map/all_gather | solution.py:91
  413.8 0.2 bitcast_reduce_fusion
  414.0 0.1 copy.199
  414.1 3.0 gather_fusion.5
  417.2 0.9 fusion.21
  418.0 57.1 %reduce-scatter.5.cloned.1.call-done = bf16[1,8,128,128]{3,2,1,0:T(8,128)(2,1)} async-done(((bf16[16,8,128,128]{3,2,1,0:T(8,128)(2,1)}), bf16[1,8,128,128]{3,2,1,0:T(8,128)(2,1)}) %reduce-scatter.5.cloned.1.call-update) | async-done | bytes 262160 | tf_op jit(solution)/shard_map/reduce_scatter | solution.py:79
  475.1 1.2 fusion.10
  476.3 0.9 fusion.20
  477.2 24.7 %all_gather.23 = bf16[16,128,128]{2,1,0:T(8,128)(2,1)S(1)} all-gather(bf16[1,128,128]{2,1,0:T(8,128)(2,1)S(1)} %copy.199), channel_id=1, replica_groups=mesh['prow'=8,'pcol'=16] {'pcol'}, dimensions={0}, use_global_device_ids=true | all-gather | bytes 557056 | tf_op jit(solution)/shard_map/all_gather | solution.py:97
  501.9 44.9 %all-reduce.6.cloned.1.call-done = (bf16[1,128,128]{2,1,0:T(8,128)(2,1)}, bf16[1,128,128]{1,2,0:T(8,128)(2,1)}) async-done(((bf16[1,128,128]{2,1,0:T(8,128)(2,1)}, bf16[1,128,128]{1,2,0:T(8,128)(2,1)}), (bf16[1,128,128]{2,1,0:T(8,128)(2,1)}, bf16[1,128,128]{1,2,0:T(8,128)(2,1)})) %all-reduce.6.cloned.1.call-update) | async-done | bytes 65552 | tf_op jit(solution)/shard_map/psum | solution.py:114
  546.8 0.9 fusion.16
  547.7 1.0 fusion.15
  548.7 0.7 copy.200
  (71 shorter events, 1.4 us)
Async XLA Ops:
  7.2 468.0 %copy-start = (bf16[1,128,128]{2,1,0:T(8,128)(2,1)S(1)}, bf16[1,128,128]{2,1,0:T(8,128)(2,1)}, u32[]{:S(2)}) copy-start(bf16[1,128,128]{2,1,0:T(8,128)(2,1)} %param.18) | copy-start | bytes 98308
  7.2 55.4 %all-gather.5.cloned.1.call-start = ((), (), s32[]{:S(2)}) async-start(), calls=%async_computation.4 | async-start | bytes 2359296 | tf_op jit(solution)/shard_map/all_gather | solution.py:65
  71.8 8.7 %copy-start.11 = (s32[16]{0:T(128)S(1)}, s32[16]{0:T(128)}, u32[]{:S(2)}) copy-start(s32[16]{0:T(128)} %param.15) | copy-start | bytes 196
  71.8 8.7 %copy-start.1 = (s32[16,64]{1,0:T(8,128)S(1)}, s32[16,64]{1,0:T(8,128)}, u32[]{:S(2)}) copy-start(s32[16,64]{1,0:T(8,128)} %param.12) | copy-start | bytes 12292
  71.8 9.3 %copy-start.10 = (s32[16,64]{1,0:T(8,128)S(1)}, s32[16,64]{1,0:T(8,128)}, u32[]{:S(2)}) copy-start(s32[16,64]{1,0:T(8,128)} %param.16) | copy-start | bytes 12292
  71.8 64.0 %all-to-all-start = ((bf16[16,1,8,128,128]{4,3,2,1,0:T(8,128)(2,1)}), bf16[16,1,8,128,128]{4,3,2,1,0:T(8,128)(2,1)}, u32[]{:S(2)}, u32[]{:S(2)}) async-start(bf16[16,1,8,128,128]{4,3,2,1,0:T(8,128)(2,1)} %broadcast_select_fusion.1), calls=%async_computation | async-start | bytes 8388608 | tf_op jit(solution)/shard_map/all_to_all | solution.py:67
  80.4 159.4 %reduce-scatter.3.cloned.1.call-start = ((), (), s32[]{:S(2)}) async-start(), calls=%async_computation.5 | async-start | bytes 4456448 | tf_op jit(solution)/shard_map/reduce_scatter | solution.py:69
  153.5 137.9 %all-gather.7.cloned.1.call-start = ((), (), s32[]{:S(2)}) async-start(), calls=%async_computation.6 | async-start | bytes 2359296 | tf_op jit(solution)/shard_map/all_gather | solution.py:75
  154.2 259.9 %all-gather.9.cloned.1.call-start = ((), (), s32[]{:S(2)}) async-start(), calls=%async_computation.8 | async-start | bytes 4456448 | tf_op jit(solution)/shard_map/all_gather | solution.py:96
  300.5 69.3 %all-to-all-start.1 = ((bf16[16,1,8,128,128]{4,3,2,1,0:T(8,128)(2,1)}), bf16[16,1,8,128,128]{4,3,2,1,0:T(8,128)(2,1)}, u32[]{:S(2)}, u32[]{:S(2)}) async-start(bf16[16,1,8,128,128]{4,3,2,1,0:T(8,128)(2,1)} %broadcast_select_fusion), calls=%async_computation.2 | async-start | bytes 8388608 | tf_op jit(solution)/shard_map/all_to_all | solution.py:77
  309.0 166.2 %reduce-scatter.5.cloned.1.call-start = ((), (), s32[]{:S(2)}) async-start(), calls=%async_computation.7 | async-start | bytes 4456448 | tf_op jit(solution)/shard_map/reduce_scatter | solution.py:79
  387.7 2.0 copy-start.8
  387.7 3.4 copy-start.9
  387.7 4.9 copy-start.3
  387.7 4.9 copy-start.5
  387.7 29.5 %copy-start.2 = (bf16[1,8,128,128]{3,2,1,0:T(8,128)(2,1)S(1)}, bf16[1,8,128,128]{3,2,1,0:T(8,128)(2,1)}, u32[]{:S(2)}) copy-start(bf16[1,8,128,128]{3,2,1,0:T(8,128)(2,1)} %param.17) | copy-start | bytes 786436
  387.7 159.1 %all-reduce.6.cloned.1.call-start = ((), (), s32[]{:S(2)}) async-start(), calls=%async_computation.9 | async-start | bytes 131072 | tf_op jit(solution)/shard_map/psum | solution.py:114
  414.1 135.3 %copy-start.6 = (bf16[1,128,128]{2,1,0:T(8,128)(2,1)}, bf16[1,128,128]{2,1,0:T(8,128)(2,1)S(1)}, u32[]{:S(2)}) copy-start(bf16[1,128,128]{2,1,0:T(8,128)(2,1)S(1)} %copy.199) | copy-start | bytes 98308
  476.3 73.1 %copy-start.4 = (bf16[1,8,128,128]{3,2,1,0:T(8,128)(2,1)}, bf16[1,8,128,128]{3,2,1,0:T(8,128)(2,1)S(1)}, u32[]{:S(2)}) copy-start(bf16[1,8,128,128]{3,2,1,0:T(8,128)(2,1)S(1)} %fusion.10) | copy-start | bytes 786436
  547.7 1.7 copy-start.7
Sparse Core Ops, SparseCore 0:
  9.6 52.8 all-gather.4
  153.6 86.1 reduce-scatter.2
  241.4 49.8 all-gather.6
  294.2 92.8 all-gather.8
  391.0 84.0 reduce-scatter.4
  478.1 68.7 all-reduce.5
